TPU v7x, 256 devices: a whole 4x4x8 slice. The times are simulated.
256 devices in a mesh: sub: 4 (over z_hi), row: 16 (over y, x), col: 4 (over z_lo, core).
Axes of the slice: x: 4, y: 4, z: 8 (z_hi: 4, z_lo: 2; z = z_hi * 2 + z_lo), core: 2. Of those that a mesh axis runs over, the one named last changes fastest.
Arguments:
- front_in: float32 [12288, 12288], P('row', ('sub', 'col')), as said below
- child_updates: float32 [4, 8192, 8192], P('sub', 'row', 'col'), as said below
- pattern: int32 [4, 32, 32], P('sub', 'row', 'col'), may hold values from 0 to 1, as said below
- child_map: int32 [4, 32], replicated, may hold values from 0 to 47, as said below
- pivot_inverse: float32 [1024, 1024], replicated, as said below
Outputs:
- front_out: float32 [12288, 12288], P('row', ('sub', 'col'))
Inputs may be any that keep to these rules, and one draw needn't show every extreme that they name: front_in is symmetric. Each child_updates[s] is symmetric. Each pattern[s] is symmetric. child_map[s] is strictly increasing, and child_map[s, i] // 3 equals i // 2. pivot_inverse is lower triangular with a positive diagonal.
All inputs are finite; a program needn't handle non-finite values.
Results may differ from a plain program's by a relative error of at most 0.000053.
Values sent between devices are 32-bit elements; how exact they have to be, the bound alone decides.
No kernel may reach another device: no remote copies, remote signals or barrier semaphores. Data moves between devices by JAX's collectives and lax.ppermute only.
A program may use at most 128 MiB of HBM per device.

v0:
```python
import jax
import jax.numpy as jnp
from jax import lax
from jax.sharding import PartitionSpec as P

BLK = 256
FRONT = 12288
CHILD = 8192
PANEL = 1024


def from_root(value, axis, source):
    kept = jnp.where(lax.axis_index(axis) == source, value, 0).astype(value.dtype)
    return lax.psum(kept, axis)


def times_transposed(left, right):
    return lax.dot_general(
        left,
        right,
        (((1,), (1,)), ((), ())),
        precision=lax.Precision.HIGHEST,
        preferred_element_type=jnp.float32,
    )


def shards(front_in, child_updates, pattern, child_map, pivot_inverse):
    sub_count = lax.axis_size("sub")
    row_count = lax.axis_size("row")
    col_count = lax.axis_size("col")
    groups = sub_count * col_count
    sub_id = lax.axis_index("sub")
    row_id = lax.axis_index("row")
    col_id = lax.axis_index("col")
    group_id = sub_id * col_count + col_id
    fblocks = FRONT // BLK
    cblocks = CHILD // BLK
    row_blocks = fblocks // row_count
    col_blocks = fblocks // groups
    child_rows = cblocks // row_count
    child_group = cblocks // groups
    child_cols = cblocks // col_count
    updates = child_updates[0].reshape(child_rows, BLK, child_cols, BLK)
    weights = pattern[0].astype(jnp.float32)
    masked = (updates * weights[:, None, :, None]).reshape(
        child_rows * BLK, sub_count, child_group * BLK
    )
    arrived = lax.all_to_all(
        lax.all_to_all(masked, "col", split_axis=1, concat_axis=1, tiled=True),
        "sub",
        split_axis=1,
        concat_axis=1,
        tiled=True,
    )
    rows_map = lax.dynamic_slice_in_dim(child_map, row_id * child_rows, child_rows, 1)
    cols_map = lax.dynamic_slice_in_dim(child_map, group_id * child_group, child_group, 1)
    row_targets = row_id * row_blocks + jnp.arange(row_blocks, dtype=jnp.int32)
    col_targets = group_id * col_blocks + jnp.arange(col_blocks, dtype=jnp.int32)
    row_hot = (rows_map[:, None, :] == row_targets[None, :, None]).astype(jnp.float32)
    col_hot = (cols_map[:, None, :] == col_targets[None, :, None]).astype(jnp.float32)
    pieces = arrived.reshape(child_rows, BLK, sub_count, child_group, BLK)
    spread_rows = jnp.einsum("spa,axsby->pxsby", row_hot, pieces, precision=lax.Precision.HIGHEST)
    extended = jnp.einsum("sqb,pxsby->pxqy", col_hot, spread_rows, precision=lax.Precision.HIGHEST)
    assembled = front_in + extended.reshape(row_blocks * BLK, col_blocks * BLK)
    panel_blocks = PANEL // BLK
    root_count = (panel_blocks + col_blocks - 1) // col_blocks
    gathered = []
    for owner in range(root_count):
        span_blocks = min(col_blocks, panel_blocks - owner * col_blocks)
        received_panel = from_root(assembled[:, : span_blocks * BLK], ("sub", "col"), owner)
        gathered.append(received_panel)
    panel_cols = jnp.concatenate(gathered, axis=1)
    factor = times_transposed(panel_cols, pivot_inverse)
    root_row = group_id * col_blocks // row_blocks
    column_factor = from_root(factor, "row", root_row)
    update = times_transposed(factor, column_factor)
    panel_parts = []
    for column in range(col_blocks):
        global_block = group_id * col_blocks + column
        panel_parts.append(
            lax.dynamic_slice_in_dim(
                factor, jnp.minimum(global_block, panel_blocks - 1) * BLK, BLK, 1
            )
        )
    panel_part = jnp.concatenate(panel_parts, axis=1)
    rows_global = (row_id * row_blocks * BLK + jnp.arange(row_blocks * BLK, dtype=jnp.int32)) // BLK
    cols_global = (
        group_id * col_blocks * BLK + jnp.arange(col_blocks * BLK, dtype=jnp.int32)
    ) // BLK
    below = (rows_global >= panel_blocks)[:, None]
    beyond = (cols_global >= panel_blocks)[None, :]
    result = jnp.where(below & beyond, assembled - update, jnp.where(below, panel_part, assembled))
    return result


def solution(mesh):
    in_specs = (P("row", ("sub", "col")), P("sub", "row", "col"), P("sub", "row", "col"), P(), P())
    out_specs = P("row", ("sub", "col"))
    return jax.shard_map(shards, mesh=mesh, in_specs=in_specs, out_specs=out_specs, check_vma=False)
```

profile of v0, /device:TPU:1, one launch (start us, length us, event | category | flops | bytes accessed | tf_op | source)
XLA Modules:
  0.0 483.1 jit_solution(3434529610521760695)
XLA Ops:
  6.5 0.7 convert_bitcast_fusion
  7.2 2.3 mul.52
  9.5 5.6 %mul.53 = f32[512,4,512]{2,1,0:T(4,128)} reshape(f32[2,256,8,256]{3,2,1,0:T(8,128)} %mul.52) | data formatting | bytes 8388608 | tf_op jit(solution)/shard_map/mul | solution.py:45
  15.2 5.3 %copy.11 = f32[512,4,512]{0,2,1:T(8,128)} copy(f32[512,4,512]{2,1,0:T(4,128)} %mul.53) | data formatting | bytes 8388608 | tf_op jit(solution)/shard_map/mul | solution.py:45
  20.4 5.4 %copy.10 = f32[1,512,2048]{1,2,0:T(8,128)} copy(f32[1,512,2048]{2,1,0:T(8,128)} %param.6) | data formatting | bytes 8388608 | tf_op args[1]
  25.8 6.4 %mul.54 = f32[512,4,512]{0,2,1:T(8,128)} multiply(f32[512,4,512]{0,2,1:T(8,128)} %bitcast.29, f32[512,4,512]{0,2,1:T(8,128)} %copy.11) | non-fusion elementwise | flops 1048576 | bytes 12582912 | tf_op jit(solution)/shard_map/mul | solution.py:45
  32.2 5.2 %copy.12 = f32[512,4,512]{2,0,1:T(8,128)} copy(f32[512,4,512]{0,2,1:T(8,128)} %mul.54) | data formatting | bytes 8388608 | tf_op jit(solution)/shard_map/mul | solution.py:45
  37.5 56.0 %all_to_all.10 = f32[512,4,512]{2,0,1:T(8,128)} all-to-all(f32[512,4,512]{2,0,1:T(8,128)} %copy.12), channel_id=1, replica_groups=mesh['sub'=4,'row'=16,'col'=4] {'col'}, dimensions={1} | all-to-all | bytes 8388608 | tf_op jit(solution)/shard_map/all_to_all | solution.py:49
  93.5 0.0 copy-start.2
  93.5 6.6 %all-to-all-start.1 = ((f32[512,4,512]{2,0,1:T(8,128)}), f32[512,4,512]{2,0,1:T(8,128)}, u32[]{:S(2)}, u32[]{:S(2)}) async-start(f32[512,4,512]{2,0,1:T(8,128)} %all_to_all.10), calls=%async_computation.1 | async-start | bytes 8388608 | tf_op jit(solution)/shard_map/all_to_all | solution.py:48
  100.1 0.0 all-reduce.6.cloned.1.call-start
  100.1 0.0 copy-done.2
  100.1 0.1 constant_dynamic-slice_fusion.3
  100.2 0.1 copy.14
  100.3 93.3 %all-to-all-done.1 = f32[512,4,512]{2,0,1:T(8,128)} async-done(((f32[512,4,512]{2,0,1:T(8,128)}), f32[512,4,512]{2,0,1:T(8,128)}, u32[]{:S(2)}, u32[]{:S(2)}) %all-to-all-start.1) | async-done | bytes 4194336 | tf_op jit(solution)/shard_map/all_to_all | solution.py:48
  193.6 5.9 %reshape.65 = f32[2,256,4,2,256]{4,3,1,0,2:T(2,128)} reshape(f32[512,4,512]{2,0,1:T(8,128)} %all-to-all-done.1) | data formatting | bytes 8388608 | tf_op jit(solution)/shard_map/reshape | solution.py:61
  199.5 13.8 %convolution_bitcast_fusion = f32[3,256,4,2,256]{4,0,3,1,2:T(4,128)S(1)} fusion(f32[2,256,4,2,256]{4,3,1,0,2:T(2,128)} %reshape.65, s32[3]{0:T(128)S(1)} %iota_add_fusion.3, s32[4,2]{1,0:T(4,128)S(1)} %get-tuple-element.13), kind=kOutput, calls=%fused_computation.2 | convolution fusion | flops 37748760 | bytes 10485804 | tf_op jit(solution)/shard_map/spa,axsby->pxsby/dot_general | solution.py:62
  213.3 7.4 %fusion = f32[3,256,256,3,1]{2,3,4,1,0:T(4,128)S(1)} fusion(f32[3,256,4,2,256]{4,0,3,1,2:T(4,128)S(1)} %convolution_bitcast_fusion, s32[4,2]{0,1:T(2,128)S(1)} %copy.14, s32[3]{0:T(128)S(1)} %iota_add_fusion.2), kind=kOutput, calls=%fused_computation | convolution fusion | flops 56623128 | bytes 8650796 | tf_op jit(solution)/shard_map/sqb,pxsby->pxqy/dot_general | solution.py:63
  220.7 0.0 copy-start.1
  220.7 0.6 copy.19
  221.3 1.1 copy-done.1
  222.4 1.7 broadcast_select_fusion.1
  224.1 0.0 copy-start
  224.1 1.5 copy-done
  225.6 0.9 slice_select_fusion
  226.5 0.0 all-reduce.6.cloned.1.call-update
  226.5 0.3 all-reduce.4.cloned.1.call-start
  226.8 117.0 %all-reduce.6.cloned.1.call-done = (f32[768,256]{1,0:T(8,128)}, f32[768,768]{1,0:T(8,128)}) async-done(((f32[768,256]{1,0:T(8,128)}, f32[768,768]{1,0:T(8,128)}), (f32[768,256]{1,0:T(8,128)}, f32[768,768]{1,0:T(8,128)})) %all-reduce.6.cloned.1.call-update) | async-done | bytes 3145744 | tf_op jit(solution)/shard_map/psum | solution.py:14
  343.9 14.4 %broadcast_select_fusion = (f32[768,1024]{1,0:T(8,128)}, f32[768,1024]{1,0:T(8,128)S(1)}) fusion(pred[]{:T(512)S(6)} %eq.43, f32[1024,1024]{1,0:T(8,128)} %param.9, f32[768,256]{1,0:T(8,128)} %get-tuple-element.5, f32[768,768]{1,0:T(8,128)} %get-tuple-element.6), kind=kOutput, calls=%fused_computation.10 | convolution fusion | flops 9665249280 | bytes 13631489 | tf_op jit(solution)/shard_map/dot_general | solution.py:18
  358.3 0.0 all-reduce.4.cloned.1.call-update
  358.3 1.6 constant_dynamic-slice_fusion.2
  359.9 104.4 %all-reduce.4.cloned.1.call-done = f32[768,1024]{1,0:T(8,128)} async-done(((f32[768,1024]{1,0:T(8,128)}), f32[768,1024]{1,0:T(8,128)}) %all-reduce.4.cloned.1.call-update) | async-done | bytes 3145744 | tf_op jit(solution)/shard_map/psum | solution.py:14
  464.4 11.9 %fusion.7 = f32[768,768]{1,0:T(8,128)} fusion(f32[768,768]{1,0:T(8,128)} %copy-done, f32[768,256]{1,0:T(8,128)} %get-tuple-element.10, f32[768,256]{1,0:T(8,128)} %get-tuple-element.11, f32[768,256]{1,0:T(8,128)} %get-tuple-element.9, f32[768,1024]{1,0:T(8,128)S(1)} %get-tuple-element.15, f32[768,1024]{1,0:T(8,128)} %all-reduce.4.cloned.1.call-done, ...), kind=kOutput, calls=%fused_computation.9 | convolution fusion | flops 7251296256 | bytes 13370880 | tf_op jit(solution)/shard_map/dot_general | solution.py:18
  (3 shorter events, 0.0 us)
Async XLA Ops:
  93.5 6.6 %copy-start.2 = (s32[4,32]{1,0:T(4,128)S(1)}, s32[4,32]{1,0:T(4,128)}, u32[]{:S(2)}) copy-start(s32[4,32]{1,0:T(4,128)} %param.8) | copy-start | bytes 1540
  93.5 100.1 %all-to-all-start.1 = ((f32[512,4,512]{2,0,1:T(8,128)}), f32[512,4,512]{2,0,1:T(8,128)}, u32[]{:S(2)}, u32[]{:S(2)}) async-start(f32[512,4,512]{2,0,1:T(8,128)} %all_to_all.10), calls=%async_computation.1 | async-start | bytes 8388608 | tf_op jit(solution)/shard_map/all_to_all | solution.py:48
  100.1 243.8 %all-reduce.6.cloned.1.call-start = ((), (), s32[]{:S(2)}) async-start(), calls=%async_computation.3 | async-start | bytes 6291456 | tf_op jit(solution)/shard_map/psum | solution.py:14
  220.7 1.7 copy-start.1
  224.1 1.5 copy-start
  226.5 237.8 %all-reduce.4.cloned.1.call-start = ((), (), s32[]{:S(2)}) async-start(), calls=%async_computation.2 | async-start | bytes 6291456 | tf_op jit(solution)/shard_map/psum | solution.py:14
Sparse Core Ops, SparseCore 0:
  226.7 117.1 all-reduce.5
  358.4 105.8 all-reduce.3
where the time goes:
time: 484 us; the launch traced here: 483 us
  waiting for transfers between devices  315 us (65%)
  blocking collectives  56 us (12%)
  matrix products  47.5 us (10%)
  local copies, waits for them, and re-layouts  34.6 us (7%)
  between operations  13.5 us (3%)
  other arithmetic  9.79 us (2%)
  starting transfers between devices  6.84 us (1%)
    psum x2, waiting for transfers between devices, from_root(): return lax.psum(kept, axis)  221 us
    all_to_all x1, waiting for transfers between devices, shards(): lax.all_to_all(lax.all_to_all(masked, 'col', split_axis=1, concat_axis=1,...  93.3 us
    all_to_all x1, blocking collectives, shards(): lax.all_to_all(masked, 'col', split_axis=1, concat_axis=1, tiled=True)  56 us
    dot_general x2, matrix products, times_transposed(): lax.dot_general(left, right, (((1,), (1,)), ((), ())), precision=lax.Prec...  26.3 us
    mul x4, local copies, waits for them, and re-layouts, shards(): updates * weights[:, None, :, None]  18.5 us
    dot_general x1, matrix products, shards(): jnp.einsum('spa,axsby->pxsby', row_hot, pieces, precision=lax.Precision.H...  13.8 us
  transfers between devices with their start and end apart: 3, of which 3 were waited for; matrix products, arithmetic and copies ran while one was open for 0% of the time, Pallas kernels for 0%

commit v1 on v0

--- a/solution.py
+++ b/solution.py
@@ -11,7 +11,7 @@
 
 def from_root(value, axis, source):
     kept = jnp.where(lax.axis_index(axis) == source, value, 0).astype(value.dtype)
-    return lax.psum(kept, axis)
+    return jnp.sum(lax.all_gather(kept, axis), axis=0)
 
 
 def times_transposed(left, right):

time: 484 us -> 851 us (1.76)
  waiting for transfers between devices: 315 us -> 641 us
  other arithmetic: 9.79 us -> 50.5 us
    all_gather x0 -> x3, waiting for transfers between devices: none -> 547 us  [from_root(): return jnp.sum(lax.all_gather(kept, axis), axis=0)]
    psum x2 -> x0, waiting for transfers between devices: 221 us -> none  [from_root(): return lax.psum(kept, axis)]
    reduce_sum x0 -> x3, other arithmetic: none -> 40.7 us  [from_root(): return jnp.sum(lax.all_gather(kept, axis), axis=0)]
  transfers between devices with their start and end apart: 3 -> 4, of which waited for: 3 -> 4; matrix products, arithmetic and copies ran while one was open for 0% -> 1% of each run, Pallas kernels for 0% -> 0%
where the time goes in v1:
time: 851 us; the launch traced here: 850 us
  waiting for transfers between devices  641 us (75%)
  blocking collectives  56 us (7%)
  other arithmetic  50.5 us (6%)
  matrix products  47.5 us (6%)
  local copies, waits for them, and re-layouts  34.4 us (4%)
  between operations  13.2 us (2%)
    all_gather x3, waiting for transfers between devices, from_root(): return jnp.sum(lax.all_gather(kept, axis), axis=0)  547 us
    all_to_all x1, waiting for transfers between devices, shards(): lax.all_to_all(lax.all_to_all(masked, 'col', split_axis=1, concat_axis=1,...  93.3 us
    all_to_all x1, blocking collectives, shards(): lax.all_to_all(masked, 'col', split_axis=1, concat_axis=1, tiled=True)  56 us
    reduce_sum x3, other arithmetic, from_root(): return jnp.sum(lax.all_gather(kept, axis), axis=0)  40.7 us
    dot_general x2, matrix products, times_transposed(): lax.dot_general(left, right, (((1,), (1,)), ((), ())), precision=lax.Prec...  26.3 us
    mul x4, local copies, waits for them, and re-layouts, shards(): updates * weights[:, None, :, None]  18.4 us
  transfers between devices with their start and end apart: 4, of which 4 were waited for; matrix products, arithmetic and copies ran while one was open for 1% of the time, Pallas kernels for 0%

profile of v1, /device:TPU:1, one launch (start us, length us, event | category | flops | bytes accessed | tf_op | source)
XLA Modules:
  0.0 850.0 jit_solution(13432269740062558481)
XLA Ops:
  6.5 0.7 convert_bitcast_fusion
  7.2 2.3 mul.52
  9.5 5.6 mul.53
  15.2 5.3 copy.11
  20.4 5.4 copy.10
  25.8 6.5 mul.54
  32.2 5.2 copy.12
  37.5 56.0 %all_to_all.10 = f32[512,4,512]{2,0,1:T(8,128)} all-to-all(f32[512,4,512]{2,0,1:T(8,128)} %copy.12), channel_id=1, replica_groups=mesh['sub'=4,'row'=16,'col'=4] {'col'}, dimensions={1} | all-to-all | bytes 8388608 | tf_op jit(solution)/shard_map/all_to_all | solution.py:49
  93.5 0.0 copy-start.2
  93.5 6.6 all-to-all-start.1
  100.1 0.0 all-gather.9.cloned.1.call-start
  100.1 0.0 copy-done.2
  100.1 0.1 constant_dynamic-slice_fusion.3
  100.2 0.1 copy.14
  100.3 93.3 %all-to-all-done.1 = f32[512,4,512]{2,0,1:T(8,128)} async-done(((f32[512,4,512]{2,0,1:T(8,128)}), f32[512,4,512]{2,0,1:T(8,128)}, u32[]{:S(2)}, u32[]{:S(2)}) %all-to-all-start.1) | async-done | bytes 4194336 | tf_op jit(solution)/shard_map/all_to_all | solution.py:48
  193.6 5.9 reshape.65
  199.5 13.8 %convolution_bitcast_fusion = f32[3,256,4,2,256]{4,0,3,1,2:T(4,128)S(1)} fusion(f32[2,256,4,2,256]{4,3,1,0,2:T(2,128)} %reshape.65, s32[3]{0:T(128)S(1)} %iota_add_fusion.3, s32[4,2]{1,0:T(4,128)S(1)} %get-tuple-element.11), kind=kOutput, calls=%fused_computation.2 | convolution fusion | flops 37748760 | bytes 10485804 | tf_op jit(solution)/shard_map/spa,axsby->pxsby/dot_general | solution.py:62
  213.3 7.4 fusion
  220.7 0.0 copy-start.1
  220.7 0.6 copy.19
  221.3 1.1 copy-done.1
  222.4 1.7 broadcast_select_fusion.1
  224.1 0.0 copy-start
  224.1 1.4 copy-done
  225.5 0.9 slice_select_fusion
  226.4 0.0 all-gather.9.cloned.1.call-update
  226.4 0.0 all-gather.7.cloned.1.call-start
  226.5 0.7 all-gather.7.cloned.1.call-update
  227.2 0.3 all-gather.11.cloned.1.call-start
  227.5 74.6 %all-gather.9.cloned.1.call-done = f32[12288,256]{1,0:T(8,128)} async-done(((f32[768,256]{1,0:T(8,128)}), f32[12288,256]{1,0:T(8,128)}) %all-gather.9.cloned.1.call-update) | async-done | bytes 12582928 | tf_op jit(solution)/shard_map/all_gather | solution.py:14
  302.1 6.3 reduce_sum.28
  308.4 188.2 %all-gather.7.cloned.1.call-done = f32[12288,768]{1,0:T(8,128)} async-done(((f32[768,768]{1,0:T(8,128)}), f32[12288,768]{1,0:T(8,128)}) %all-gather.7.cloned.1.call-update) | async-done | bytes 37748752 | tf_op jit(solution)/shard_map/all_gather | solution.py:14
  496.6 15.1 %reduce_sum.27 = f32[768,768]{1,0:T(8,128)} reduce(f32[16,768,768]{2,1,0:T(8,128)} %bitcast.33, f32[]{:T(128)} %constant.59.clone.1), dimensions={0}, to_apply=%region_0.1 | reduce | flops 8847360 | bytes 40108036 | tf_op jit(solution)/shard_map/reduce_sum | solution.py:14
  511.8 14.4 %broadcast_select_fusion = (f32[768,1024]{1,0:T(8,128)}, f32[768,1024]{1,0:T(8,128)S(1)}) fusion(pred[]{:T(512)S(6)} %eq.43, f32[1024,1024]{1,0:T(8,128)} %param.9, f32[768,256]{1,0:T(8,128)} %reduce_sum.28, f32[768,768]{1,0:T(8,128)} %reduce_sum.27), kind=kOutput, calls=%fused_computation.10 | convolution fusion | flops 9665249280 | bytes 13631489 | tf_op jit(solution)/shard_map/dot_general | solution.py:18
  526.1 0.0 all-gather.11.cloned.1.call-update
  526.2 1.5 constant_dynamic-slice_fusion.2
  527.7 284.6 %all-gather.11.cloned.1.call-done = f32[12288,1024]{1,0:T(8,128)} async-done(((f32[768,1024]{1,0:T(8,128)}), f32[12288,1024]{1,0:T(8,128)}) %all-gather.11.cloned.1.call-update) | async-done | bytes 50331664 | tf_op jit(solution)/shard_map/all_gather | solution.py:14
  812.3 19.2 %reduce_sum.29 = f32[768,1024]{1,0:T(8,128)} reduce(f32[16,768,1024]{2,1,0:T(8,128)} %bitcast.32, f32[]{:T(128)} %constant.59.clone.1), dimensions={0}, to_apply=%region_2.3 | reduce | flops 11796480 | bytes 53477380 | tf_op jit(solution)/shard_map/reduce_sum | solution.py:14
  831.6 11.9 %fusion.7 = f32[768,768]{1,0:T(8,128)} fusion(f32[768,768]{1,0:T(8,128)} %copy-done, f32[768,256]{1,0:T(8,128)} %get-tuple-element.8, f32[768,256]{1,0:T(8,128)} %get-tuple-element.9, f32[768,256]{1,0:T(8,128)} %get-tuple-element.7, f32[768,1024]{1,0:T(8,128)S(1)} %get-tuple-element.13, f32[768,1024]{1,0:T(8,128)} %reduce_sum.29, ...), kind=kOutput, calls=%fused_computation.9 | convolution fusion | flops 7251296256 | bytes 13370880 | tf_op jit(solution)/shard_map/dot_general | solution.py:18
  (4 shorter events, 0.0 us)
Async XLA Ops:
  93.5 6.6 copy-start.2
  93.5 100.1 %all-to-all-start.1 = ((f32[512,4,512]{2,0,1:T(8,128)}), f32[512,4,512]{2,0,1:T(8,128)}, u32[]{:S(2)}, u32[]{:S(2)}) async-start(f32[512,4,512]{2,0,1:T(8,128)} %all_to_all.10), calls=%async_computation.1 | async-start | bytes 8388608 | tf_op jit(solution)/shard_map/all_to_all | solution.py:48
  100.1 202.0 %all-gather.9.cloned.1.call-start = ((), (), s32[]{:S(2)}) async-start(), calls=%async_computation.3 | async-start | bytes 13369344 | tf_op jit(solution)/shard_map/all_gather | solution.py:14
  220.7 1.7 copy-start.1
  224.1 1.4 copy-start
  226.4 270.2 %all-gather.7.cloned.1.call-start = ((), (), s32[]{:S(2)}) async-start(), calls=%async_computation.2 | async-start | bytes 40108032 | tf_op jit(solution)/shard_map/all_gather | solution.py:14
  227.2 585.1 %all-gather.11.cloned.1.call-start = ((), (), s32[]{:S(2)}) async-start(), calls=%async_computation.4 | async-start | bytes 53477376 | tf_op jit(solution)/shard_map/all_gather | solution.py:14
Sparse Core Ops, SparseCore 0:
  226.6 75.4 all-gather.8
  303.9 192.6 all-gather.6
  526.3 286.0 all-gather.10
